TPU v7x, 512 devices: a whole 4x4x16 slice. The times are simulated.
512 devices in a mesh: tm: 128 (over y, x_hi, z), col: 4 (over x_lo, core).
Axes of the slice: x: 4 (x_hi: 2, x_lo: 2; x = x_hi * 2 + x_lo), y: 4, z: 16, core: 2. Of those that a mesh axis runs over, the one named last changes fastest.
Arguments:
- frames: bfloat16 [384, 2, 96, 384], P('tm', None, 'col'), may hold values from -6 to 6
- up_kernel: bfloat16 [10368, 256], P(None, 'tm'), may hold values from -0.109375 to 0.109375
- mix_kernel: bfloat16 [6912, 256], P(None, 'tm'), may hold values from -0.078125 to 0.078125
- cotangent: bfloat16 [768, 2, 96, 256], P('tm', None, 'col'), may hold values from -6 to 6
Outputs:
- decoded: bfloat16 [768, 2, 96, 256], P('tm', None, 'col')
- frames_grad: bfloat16 [384, 2, 96, 384], P('tm', None, 'col')
All inputs are finite; a program needn't handle non-finite values.
Results may differ from a plain program's by a relative error of at most 0.005.
Values may be sent and summed in bfloat16 or wider, within the bound.
No kernel may reach another device: no remote copies, remote signals or barrier semaphores. Data moves between devices by JAX's collectives and lax.ppermute only.
A program may use at most 64 MiB of HBM per device.

v0:
```python
import jax
import jax.numpy as jnp
from jax import lax
from jax.sharding import PartitionSpec as P


def with_halo(block, sides, width):
    for axis, dim in sides:
        count = lax.axis_size(axis)
        forward = [(i, i + 1) for i in range(count - 1)]
        backward = [(target, source) for source, target in forward]
        low = lax.ppermute(
            lax.slice_in_dim(block, block.shape[dim] - width, None, axis=dim), axis, forward
        )
        high = lax.ppermute(lax.slice_in_dim(block, 0, width, axis=dim), axis, backward)
        block = jnp.concatenate([low, block, high], axis=dim)
    return block


def from_behind(array, axis, by):
    devices = lax.axis_size(axis)
    pairs = [(i, i + by) for i in range(devices) if 0 <= i + by < devices]
    return lax.ppermute(array, axis, pairs)


def widen(field):
    return with_halo(field, (("col", 2),), 1)


def from_previous(field):
    return from_behind(field, "tm", 1)


def from_next(field):
    return from_behind(field, "tm", -1)


def forward_pass(kernel, produce):
    return produce(lax.all_gather(kernel, "tm", axis=1, tiled=True), jnp.int32(0))


def backward_pass(kernel, combine, initial):
    return combine(initial, lax.all_gather(kernel, "tm", axis=1, tiled=True), jnp.int32(0))


def pad_rows(field):
    return jnp.pad(field, ((0, 0), (1, 1), (0, 0), (0, 0)))


def window(padded, first, count, row_low, col_low, height, width):
    part = padded[first : first + count, row_low : row_low + height, col_low : col_low + width]
    return part.reshape(-1, part.shape[-1])


def transposed(rows, matrix):
    return lax.dot_general(
        rows, matrix, (((1,), (1,)), ((), ())), preferred_element_type=jnp.float32
    )


def shards(frames, up_kernel, mix_kernel, cotangent):
    frame_count, height, width, in_channels = frames.shape
    out_channels = mix_kernel.shape[0] // 27
    count = 2 * frame_count
    block = count * height * width
    widened = widen(frames)
    earlier = from_previous(widened[-1:])
    extended = pad_rows(jnp.concatenate((earlier, widened), axis=0))
    rows_in = extended.shape[0] - 1

    def up_columns(piece, start):
        taps = piece.reshape(3, 3, 3, in_channels, piece.shape[1])
        even = jnp.zeros((rows_in * height * width, piece.shape[1]), jnp.float32)
        odd = even
        for tap_h in range(3):
            for tap_w in range(3):
                current = window(extended, 1, rows_in, tap_h, tap_w, height, width)
                prior = window(extended, 0, rows_in, tap_h, tap_w, height, width)
                even = even + jnp.dot(
                    current, taps[0, tap_h, tap_w], preferred_element_type=jnp.float32
                )
                even = even + jnp.dot(
                    prior, taps[2, tap_h, tap_w], preferred_element_type=jnp.float32
                )
                odd = odd + jnp.dot(
                    current, taps[1, tap_h, tap_w], preferred_element_type=jnp.float32
                )
        stacked = jnp.stack(
            (even.reshape(rows_in, height * width, -1), odd.reshape(rows_in, height * width, -1)),
            axis=1,
        )
        return stacked.reshape(-1, piece.shape[1])

    before_all = forward_pass(up_kernel, up_columns).reshape(
        2 * rows_in, height, width, out_channels
    )
    hidden = jax.nn.silu(before_all).astype(jnp.bfloat16)
    earlier_hidden = from_previous(hidden[-2:])
    hidden_pad = pad_rows(widen(jnp.concatenate((earlier_hidden, hidden), axis=0)))
    cot_pad = pad_rows(widen(jnp.concatenate((cotangent, from_next(cotangent[:2])), axis=0)))

    def mix_forward(piece, start):
        taps = piece.reshape(3, 3, 3, out_channels, piece.shape[1])
        total = jnp.zeros((block, piece.shape[1]), jnp.float32)
        for tap_t in range(3):
            for tap_h in range(3):
                for tap_w in range(3):
                    total = total + jnp.dot(
                        window(hidden_pad, tap_t, count, tap_h, tap_w, height, width),
                        taps[tap_t, tap_h, tap_w],
                        preferred_element_type=jnp.float32,
                    )
        return total

    def mix_backward(piece):
        taps = piece.reshape(3, 3, 3, out_channels, piece.shape[1])
        total = jnp.zeros((block, out_channels), jnp.float32)
        for tap_t in range(3):
            for tap_h in range(3):
                for tap_w in range(3):
                    total = total + transposed(
                        window(cot_pad, 2 - tap_t, count, 2 - tap_h, 2 - tap_w, height, width),
                        taps[tap_t, tap_h, tap_w],
                    )
        return total

    empty = jnp.zeros((block, out_channels), jnp.float32)
    decoded_flat = forward_pass(mix_kernel, mix_forward)

    def accumulate(total, piece, start):
        return mix_backward(piece)

    hidden_grad = backward_pass(mix_kernel, accumulate, empty)
    flat_before = before_all.reshape(block, out_channels)
    sigma = jax.nn.sigmoid(flat_before)
    before_grad = (hidden_grad * sigma * (1.0 + flat_before * (1.0 - sigma))).astype(jnp.bfloat16)
    before_grad = before_grad.reshape(count, height, width, out_channels)
    grad_pad = pad_rows(widen(jnp.concatenate((before_grad, from_next(before_grad[:1])), axis=0)))
    evens = grad_pad[0::2]
    odds = grad_pad[1::2]

    def up_backward(total, piece, start):
        taps = piece.reshape(3, 3, 3, in_channels, piece.shape[1])
        for tap_h in range(3):
            for tap_w in range(3):
                total = total + transposed(
                    window(evens, 0, frame_count, 2 - tap_h, 2 - tap_w, height, width),
                    taps[0, tap_h, tap_w],
                )
                total = total + transposed(
                    window(odds, 0, frame_count, 2 - tap_h, 2 - tap_w, height, width),
                    taps[1, tap_h, tap_w],
                )
                total = total + transposed(
                    window(evens, 1, frame_count, 2 - tap_h, 2 - tap_w, height, width),
                    taps[2, tap_h, tap_w],
                )
        return total

    grad_start = jnp.zeros((frame_count * height * width, in_channels), jnp.float32)
    grad_total = backward_pass(up_kernel, up_backward, grad_start)
    decoded = decoded_flat.astype(jnp.bfloat16).reshape(count, height, width, out_channels)
    frames_grad = grad_total.astype(jnp.bfloat16).reshape(frame_count, height, width, in_channels)
    return (decoded, frames_grad)


def solution(mesh):
    placed = (P("tm", None, "col", None), P(None, "tm"), P(None, "tm"), P("tm", None, "col", None))
    return jax.shard_map(
        shards,
        mesh=mesh,
        in_specs=placed,
        out_specs=(P("tm", None, "col", None), P("tm", None, "col", None)),
        check_vma=False,
    )
```

profile of v0, /device:TPU:1, one launch (start us, length us, event | category | flops | bytes accessed | tf_op | source)
XLA Modules:
  0.0 542.3 jit_solution(755618982540305264)
XLA Ops:
  9.5 8.8 %collective-permute-start.1 = (bf16[3,2,1,384]{3,2,1,0:T(2,128)(2,1)S(1)}, bf16[3,2,1,384]{3,2,1,0:T(2,128)(2,1)S(1)}, u32[]{:S(2)}, u32[]{:S(2)}) collective-permute-start(bf16[3,2,1,384]{3,2,1,0:T(2,128)(2,1)S(1)} %get-tuple-element.114), channel_id=1, source_target_pairs={{1,0},{2,1},{3,2},{5,4},{6,5},{7,6},{9,8},{10,9},{11,10},{13,12},{... | collective-permute-start | bytes 13832 | tf_op jit(solution)/shard_map/ppermute | solution.py:15
  18.3 1.9 collective-permute-start
  21.0 1.3 collective-permute-start.6
  22.3 0.9 constant_dynamic-update-slice_fusion.1
  24.0 4.0 collective-permute-start.2
  28.0 1.7 pad_maximum_fusion.5
  29.8 1.0 maximum_maximum_fusion.1
  30.8 3.0 collective-permute-start.8
  33.8 2.6 collective-permute-start.7
  36.4 1.2 pad_slice_fusion
  37.8 1.1 pad_maximum_fusion.2
  38.9 1.5 fusion.45
  40.5 188.4 %all-gather.7.cloned.1.call-done = bf16[128,2,6912]{2,1,0:T(2,128)(2,1)} async-done(((bf16[1,2,6912]{2,1,0:T(2,128)(2,1)}), bf16[128,2,6912]{2,1,0:T(2,128)(2,1)}) %all-gather.7.cloned.1.call-update) | async-done | bytes 3538960 | tf_op jit(solution)/shard_map/all_gather | solution.py:39
  228.9 8.3 %reshape.429 = bf16[256,6912]{1,0:T(8,128)(2,1)} reshape(bf16[128,2,6912]{2,1,0:T(2,128)(2,1)} %all-gather.7.cloned.1.call-done) | data formatting | bytes 7077888
  237.1 5.0 copy.18
  242.2 1.2 fusion.44
  243.4 1.2 fusion.43
  244.6 1.2 fusion.41
  245.8 1.1 fusion.40
  246.9 1.2 fusion.38
  248.1 1.1 convolution_add_fusion.21
  249.2 1.2 convolution_add_fusion.20
  250.4 1.2 convolution_add_fusion.19
  255.8 0.9 convolution_add_fusion.1
  256.8 200.9 %all-gather.5.cloned.1.call-done = bf16[128,2,10368]{2,1,0:T(2,128)(2,1)} async-done(((bf16[1,2,10368]{2,1,0:T(2,128)(2,1)}), bf16[128,2,10368]{2,1,0:T(2,128)(2,1)}) %all-gather.5.cloned.1.call-update) | async-done | bytes 5308432 | tf_op jit(solution)/shard_map/all_gather | solution.py:39
  457.7 7.9 %reshape.427 = bf16[256,10368]{1,0:T(8,128)(2,1)} reshape(bf16[128,2,10368]{2,1,0:T(2,128)(2,1)} %all-gather.5.cloned.1.call-done) | data formatting | bytes 10616832
  465.6 8.0 %copy.15 = bf16[10368,256]{1,0:T(8,128)(2,1)} copy(bf16[10368,256]{0,1:T(8,128)(2,1)} %bitcast.565) | data formatting | bytes 10616832
  473.7 1.3 fusion.30
  475.0 1.7 fusion.27
  476.7 1.2 fusion.32
  477.9 1.2 fusion.31
  479.1 1.2 fusion.29
  480.3 1.2 fusion.28
  481.5 1.2 convolution_add_fusion.78
  482.7 1.2 convolution_add_fusion.93
  483.9 1.2 convolution_add_fusion.92
  485.1 1.2 convolution_add_fusion.77
  486.3 1.2 convolution_add_fusion.91
  491.3 1.3 collective-permute-start.9
  492.6 3.3 collective-permute-done.9
  495.9 12.7 %collective-permute-start.11 = (bf16[7,2,1,256]{3,2,1,0:T(2,128)(2,1)S(1)}, bf16[7,2,1,256]{3,2,1,0:T(2,128)(2,1)S(1)}, u32[]{:S(2)}, u32[]{:S(2)}) collective-permute-start(bf16[7,2,1,256]{3,2,1,0:T(2,128)(2,1)S(1)} %get-tuple-element.110), channel_id=1, source_target_pairs={{1,0},{2,1},{3,2},{5,4},{6,5},{7,6},{9,8},{10,9},{11,10},{13,12},{... | collective-permute-start | bytes 21512 | tf_op jit(solution)/shard_map/ppermute | solution.py:15
  508.7 2.1 collective-permute-start.10
  510.9 2.9 collective-permute-start.3
  520.1 0.9 fusion.9
  521.0 2.7 collective-permute-start.4
  523.7 1.9 collective-permute-start.5
  525.7 3.1 collective-permute-done.5
  534.6 0.9 fusion.7
  (189 shorter events, 23.5 us)
Async XLA Ops:
  7.2 221.7 %all-gather.7.cloned.1.call-start = ((), (), s32[]{:S(2)}) async-start(), calls=%async_computation.1 | async-start | bytes 3566592 | tf_op jit(solution)/shard_map/all_gather | solution.py:39
  7.9 449.8 %all-gather.5.cloned.1.call-start = ((), (), s32[]{:S(2)}) async-start(), calls=%async_computation | async-start | bytes 5349888 | tf_op jit(solution)/shard_map/all_gather | solution.py:39
  9.5 13.7 %collective-permute-start.1 = (bf16[3,2,1,384]{3,2,1,0:T(2,128)(2,1)S(1)}, bf16[3,2,1,384]{3,2,1,0:T(2,128)(2,1)S(1)}, u32[]{:S(2)}, u32[]{:S(2)}) collective-permute-start(bf16[3,2,1,384]{3,2,1,0:T(2,128)(2,1)S(1)} %get-tuple-element.114), channel_id=1, source_target_pairs={{1,0},{2,1},{3,2},{5,4},{6,5},{7,6},{9,8},{10,9},{11,10},{13,12},{... | collective-permute-start | bytes 13832 | tf_op jit(solution)/shard_map/ppermute | solution.py:15
  18.3 5.0 collective-permute-start
  21.0 9.8 %collective-permute-start.6 = (bf16[2,2,24,256]{3,2,1,0:T(8,128)(2,1)S(1)}, bf16[2,2,24,256]{3,2,1,0:T(8,128)(2,1)S(1)}, u32[]{:S(2)}, u32[]{:S(2)}) collective-permute-start(bf16[2,2,24,256]{3,2,1,0:T(8,128)(2,1)S(1)} %slice.702), channel_id=1, source_target_pairs={{4,0},{8,4},{12,8},{16,12},{20,16},{24,20},{28,24},{32,28},{36,32}... | collective-permute-start | bytes 147464 | tf_op jit(solution)/shard_map/ppermute | solution.py:23
  24.0 5.7 %collective-permute-start.2 = (bf16[1,2,26,384]{3,2,1,0:T(8,128)(2,1)S(1)}, bf16[1,2,26,384]{3,2,1,0:T(8,128)(2,1)S(1)}, u32[]{:S(2)}, u32[]{:S(2)}) collective-permute-start(bf16[1,2,26,384]{3,2,1,0:T(8,128)(2,1)S(1)} %pad_maximum_fusion.7), channel_id=1, source_target_pairs={{0,4},{4,8},{8,12},{12,16},{16,20},{20,24},{24,28},{28,32},{32,36}... | collective-permute-start | bytes 119816 | tf_op jit(solution)/shard_map/ppermute | solution.py:23
  30.8 6.8 %collective-permute-start.8 = (bf16[8,2,1,256]{3,2,1,0:T(2,128)(2,1)S(1)}, bf16[8,2,1,256]{3,2,1,0:T(2,128)(2,1)S(1)}, u32[]{:S(2)}, u32[]{:S(2)}) collective-permute-start(bf16[8,2,1,256]{3,2,1,0:T(2,128)(2,1)S(1)} %get-tuple-element.87), channel_id=1, source_target_pairs={{1,0},{2,1},{3,2},{5,4},{6,5},{7,6},{9,8},{10,9},{11,10},{13,12},{... | collective-permute-start | bytes 24584 | tf_op jit(solution)/shard_map/ppermute | solution.py:15
  33.8 3.9 collective-permute-start.7
  242.1 9.5 %copy-start.12 = (bf16[6,2,24,256]{3,2,1,0:T(8,128)(2,1)S(1)}, bf16[6,2,24,256]{3,2,1,0:T(8,128)(2,1)}, u32[]{:S(2)}) copy-start(bf16[6,2,24,256]{3,2,1,0:T(8,128)(2,1)} %get-tuple-element.85) | copy-start | bytes 442372
  242.1 9.7 %copy-start.27 = (bf16[6,2,24,256]{3,2,1,0:T(8,128)(2,1)S(1)}, bf16[6,2,24,256]{3,2,1,0:T(8,128)(2,1)}, u32[]{:S(2)}) copy-start(bf16[6,2,24,256]{3,2,1,0:T(8,128)(2,1)} %get-tuple-element.16) | copy-start | bytes 442372
  242.1 10.0 %copy-start.26 = (bf16[6,2,24,256]{3,2,1,0:T(8,128)(2,1)S(1)}, bf16[6,2,24,256]{3,2,1,0:T(8,128)(2,1)}, u32[]{:S(2)}) copy-start(bf16[6,2,24,256]{3,2,1,0:T(8,128)(2,1)} %get-tuple-element.15) | copy-start | bytes 442372
  242.1 10.2 %copy-start.25 = (bf16[6,2,24,256]{3,2,1,0:T(8,128)(2,1)S(1)}, bf16[6,2,24,256]{3,2,1,0:T(8,128)(2,1)}, u32[]{:S(2)}) copy-start(bf16[6,2,24,256]{3,2,1,0:T(8,128)(2,1)} %get-tuple-element.14) | copy-start | bytes 442372
  242.1 10.5 %copy-start.24 = (bf16[6,2,24,256]{3,2,1,0:T(8,128)(2,1)S(1)}, bf16[6,2,24,256]{3,2,1,0:T(8,128)(2,1)}, u32[]{:S(2)}) copy-start(bf16[6,2,24,256]{3,2,1,0:T(8,128)(2,1)} %get-tuple-element.13) | copy-start | bytes 442372
  242.2 10.7 %copy-start.23 = (bf16[6,2,24,256]{3,2,1,0:T(8,128)(2,1)S(1)}, bf16[6,2,24,256]{3,2,1,0:T(8,128)(2,1)}, u32[]{:S(2)}) copy-start(bf16[6,2,24,256]{3,2,1,0:T(8,128)(2,1)} %get-tuple-element.12) | copy-start | bytes 442372
  243.4 9.7 %copy-start.22 = (bf16[6,2,24,256]{3,2,1,0:T(8,128)(2,1)S(1)}, bf16[6,2,24,256]{3,2,1,0:T(8,128)(2,1)}, u32[]{:S(2)}) copy-start(bf16[6,2,24,256]{3,2,1,0:T(8,128)(2,1)} %get-tuple-element.11) | copy-start | bytes 442372
  244.6 8.8 %copy-start.13 = (bf16[6,2,24,256]{3,2,1,0:T(8,128)(2,1)S(1)}, bf16[6,2,24,256]{3,2,1,0:T(8,128)(2,1)}, u32[]{:S(2)}) copy-start(bf16[6,2,24,256]{3,2,1,0:T(8,128)(2,1)} %get-tuple-element.81) | copy-start | bytes 442372
  246.9 6.7 %copy-start.11 = (bf16[6,2,24,256]{3,2,1,0:T(8,128)(2,1)S(1)}, bf16[6,2,24,256]{3,2,1,0:T(8,128)(2,1)}, u32[]{:S(2)}) copy-start(bf16[6,2,24,256]{3,2,1,0:T(8,128)(2,1)} %get-tuple-element.84) | copy-start | bytes 442372
  249.2 4.6 copy-start.21
  250.4 3.7 copy-start.20
  251.6 2.8 copy-start.19
  251.6 3.0 copy-start.18
  251.9 3.0 copy-start.17
  252.1 3.0 copy-start.16
  252.4 2.9 copy-start.10
  252.9 2.7 copy-start.9
  253.1 2.7 copy-start.15
  473.6 13.9 %copy-start = (bf16[10368,256]{1,0:T(8,128)(2,1)S(1)}, bf16[10368,256]{1,0:T(8,128)(2,1)}, u32[]{:S(2)}) copy-start(bf16[10368,256]{1,0:T(8,128)(2,1)} %copy.15) | copy-start | bytes 15925252
  473.6 13.9 %copy-start.6 = (bf16[3,2,24,384]{3,2,1,0:T(8,128)(2,1)S(1)}, bf16[3,2,24,384]{3,2,1,0:T(8,128)(2,1)}, u32[]{:S(2)}) copy-start(bf16[3,2,24,384]{3,2,1,0:T(8,128)(2,1)} %get-tuple-element.98) | copy-start | bytes 331780
  473.6 14.1 %copy-start.32 = (bf16[3,2,24,384]{3,2,1,0:T(8,128)(2,1)S(1)}, bf16[3,2,24,384]{3,2,1,0:T(8,128)(2,1)}, u32[]{:S(2)}) copy-start(bf16[3,2,24,384]{3,2,1,0:T(8,128)(2,1)} %get-tuple-element.99) | copy-start | bytes 331780
  473.6 14.3 %copy-start.8 = (bf16[3,2,24,384]{3,2,1,0:T(8,128)(2,1)S(1)}, bf16[3,2,24,384]{3,2,1,0:T(8,128)(2,1)}, u32[]{:S(2)}) copy-start(bf16[3,2,24,384]{3,2,1,0:T(8,128)(2,1)} %get-tuple-element.112) | copy-start | bytes 331780
  473.6 14.6 %copy-start.1 = (bf16[3,2,24,384]{3,2,1,0:T(8,128)(2,1)S(1)}, bf16[3,2,24,384]{3,2,1,0:T(8,128)(2,1)}, u32[]{:S(2)}) copy-start(bf16[3,2,24,384]{3,2,1,0:T(8,128)(2,1)} %param.4) | copy-start | bytes 331780
  473.6 14.8 %copy-start.31 = (bf16[3,2,24,384]{3,2,1,0:T(8,128)(2,1)S(1)}, bf16[3,2,24,384]{3,2,1,0:T(8,128)(2,1)}, u32[]{:S(2)}) copy-start(bf16[3,2,24,384]{3,2,1,0:T(8,128)(2,1)} %get-tuple-element.106) | copy-start | bytes 331780
  473.6 15.0 %copy-start.7 = (bf16[3,2,24,384]{3,2,1,0:T(8,128)(2,1)S(1)}, bf16[3,2,24,384]{3,2,1,0:T(8,128)(2,1)}, u32[]{:S(2)}) copy-start(bf16[3,2,24,384]{3,2,1,0:T(8,128)(2,1)} %get-tuple-element.111) | copy-start | bytes 331780
  473.6 15.2 %copy-start.3 = (bf16[3,2,24,384]{3,2,1,0:T(8,128)(2,1)S(1)}, bf16[3,2,24,384]{3,2,1,0:T(8,128)(2,1)}, u32[]{:S(2)}) copy-start(bf16[3,2,24,384]{3,2,1,0:T(8,128)(2,1)} %get-tuple-element.100) | copy-start | bytes 331780
  477.9 11.5 %copy-start.5 = (bf16[3,2,24,384]{3,2,1,0:T(8,128)(2,1)S(1)}, bf16[3,2,24,384]{3,2,1,0:T(8,128)(2,1)}, u32[]{:S(2)}) copy-start(bf16[3,2,24,384]{3,2,1,0:T(8,128)(2,1)} %get-tuple-element.102) | copy-start | bytes 331780
  479.1 10.5 %copy-start.30 = (bf16[3,2,24,384]{3,2,1,0:T(8,128)(2,1)S(1)}, bf16[3,2,24,384]{3,2,1,0:T(8,128)(2,1)}, u32[]{:S(2)}) copy-start(bf16[3,2,24,384]{3,2,1,0:T(8,128)(2,1)} %get-tuple-element.101) | copy-start | bytes 331780
  481.5 8.5 %copy-start.4 = (bf16[3,2,24,384]{3,2,1,0:T(8,128)(2,1)S(1)}, bf16[3,2,24,384]{3,2,1,0:T(8,128)(2,1)}, u32[]{:S(2)}) copy-start(bf16[3,2,24,384]{3,2,1,0:T(8,128)(2,1)} %get-tuple-element.104) | copy-start | bytes 331780
  482.7 7.5 %copy-start.29 = (bf16[3,2,24,384]{3,2,1,0:T(8,128)(2,1)S(1)}, bf16[3,2,24,384]{3,2,1,0:T(8,128)(2,1)}, u32[]{:S(2)}) copy-start(bf16[3,2,24,384]{3,2,1,0:T(8,128)(2,1)} %get-tuple-element.103) | copy-start | bytes 331780
  485.1 5.5 %copy-start.28 = (bf16[3,2,24,384]{3,2,1,0:T(8,128)(2,1)S(1)}, bf16[3,2,24,384]{3,2,1,0:T(8,128)(2,1)}, u32[]{:S(2)}) copy-start(bf16[3,2,24,384]{3,2,1,0:T(8,128)(2,1)} %get-tuple-element.94) | copy-start | bytes 331780
  488.0 3.1 copy-start.2
  488.0 3.1 copy-start.14
  491.3 4.6 collective-permute-start.9
  495.9 17.9 %collective-permute-start.11 = (bf16[7,2,1,256]{3,2,1,0:T(2,128)(2,1)S(1)}, bf16[7,2,1,256]{3,2,1,0:T(2,128)(2,1)S(1)}, u32[]{:S(2)}, u32[]{:S(2)}) collective-permute-start(bf16[7,2,1,256]{3,2,1,0:T(2,128)(2,1)S(1)} %get-tuple-element.110), channel_id=1, source_target_pairs={{1,0},{2,1},{3,2},{5,4},{6,5},{7,6},{9,8},{10,9},{11,10},{13,12},{... | collective-permute-start | bytes 21512 | tf_op jit(solution)/shard_map/ppermute | solution.py:15
  508.7 5.1 collective-permute-start.10
  510.9 10.1 %collective-permute-start.3 = (bf16[2,2,24,256]{3,2,1,0:T(8,128)(2,1)S(1)}, bf16[2,2,24,256]{3,2,1,0:T(8,128)(2,1)S(1)}, u32[]{:S(2)}, u32[]{:S(2)}) collective-permute-start(bf16[2,2,24,256]{3,2,1,0:T(8,128)(2,1)S(1)} %slice.794), channel_id=1, source_target_pairs={{0,4},{4,8},{8,12},{12,16},{16,20},{20,24},{24,28},{28,32},{32,36}... | collective-permute-start | bytes 147464 | tf_op jit(solution)/shard_map/ppermute | solution.py:23
  521.0 4.7 collective-permute-start.4
  523.7 5.1 collective-permute-start.5
Sparse Core Ops, SparseCore 0:
  12.5 216.3 all-gather.6
  233.4 224.2 all-gather.4
where the time goes:
time: 544 us; the launch traced here: 542 us
  waiting for transfers between devices  397 us (73%)
  starting transfers between devices  45.2 us (8%)
  matrix products  43.6 us (8%)
  local copies, waits for them, and re-layouts  35.3 us (6%)
  between operations  15.6 us (3%)
  other arithmetic  5.54 us (1%)
    all_gather x2, waiting for transfers between devices, forward_pass(): lax.all_gather(kernel, 'tm', axis=1, tiled=True)  389 us
    unnamed x71, local copies, waits for them, and re-layouts  30.2 us
    ppermute x4, starting transfers between devices, with_halo(): lax.ppermute(lax.slice_in_dim(block, 0, width, axis=dim), axis, backward)  26.4 us
    dot_general x54, matrix products, transposed(): lax.dot_general(rows, matrix, (((1,), (1,)), ((), ())), preferred_element...  21 us
  transfers between devices with their start and end apart: 14, of which 4 were waited for; matrix products, arithmetic and copies ran while one was open for 8% of the time, Pallas kernels for 0%

commit v1 on v0

v1 whole, which is shorter than its diff:
```python
import jax
import jax.numpy as jnp
from jax import lax
from jax.sharding import Mesh, PartitionSpec as P

PLANES = ("y", "xh", "z")
COLS = ("xl", "core")
LANES = 128


def shift(array, axis, by):
    devices = lax.axis_size(axis)
    pairs = [(i, i + by) for i in range(devices) if 0 <= i + by < devices]
    return lax.ppermute(array, axis, pairs)


def cross(array):
    return lax.ppermute(array, ("xh", "xl"), [(0, 3), (3, 0), (1, 2), (2, 1)])


def swap(array):
    return lax.ppermute(array, "core", [(0, 1), (1, 0)])


def spread(array, axis):
    count = lax.axis_size(axis)
    return lax.all_to_all(
        jnp.broadcast_to(array, (count, *array.shape)), axis, 0, 0, tiled=True
    )


def gather(tiles):
    planes = spread(tiles, "z")
    depth = planes.shape[0]
    rows = planes.transpose(1, 0, 2, 3).reshape(tiles.shape[0], 2 * depth, LANES)
    return spread(rows, "y")


def convolve(field, kernel, strides=(1, 1, 1)):
    return lax.conv_general_dilated(
        field,
        kernel,
        strides,
        ((0, 0), (1, 1), (0, 0)),
        dimension_numbers=("NDHWC", "DHWIO", "NDHWC"),
        preferred_element_type=jnp.float32,
    )


def with_columns(field):
    width = field.shape[2]
    low = shift(field[:, :, width - 2 :], COLS, 1)
    high = shift(field[:, :, :2], COLS, -1)
    return jnp.concatenate((low, field, high), axis=2)


def tiles_of(kernel):
    return kernel.T.reshape(2, -1, LANES).transpose(1, 0, 2)


def shards(frames, up_kernel, mix_kernel, cotangent):
    frame_count, height, width, in_channels = frames.shape
    out_channels = mix_kernel.shape[0] // 27
    half = out_channels // 2
    xh, xl, core = lax.axis_index("xh"), lax.axis_index("xl"), lax.axis_index("core")
    planes_y, planes_z = lax.axis_size("y"), lax.axis_size("z")
    run = out_channels // planes_y // 2

    mix_other = cross(tiles_of(mix_kernel))
    up_tiles = tiles_of(up_kernel)
    up_count = up_tiles.shape[0]
    up_half = (up_count + 1) // 2
    up_part = lax.dynamic_slice_in_dim(up_tiles, core * (up_count - up_half), up_half, 0)
    up_rows = gather(up_part)

    mix_tiles = jnp.where(xh == core, tiles_of(mix_kernel), mix_other)
    source = lax.broadcasted_iota(jnp.int32, (out_channels, half), 0)
    target = lax.broadcasted_iota(jnp.int32, (out_channels, half), 1)
    wanted = (target // run) * (2 * run) + xh * run + target % run
    pick = (source == wanted).astype(jnp.bfloat16).reshape(-1, LANES, half)
    mix_part = jnp.einsum(
        "ktjl,tlm->kjm",
        mix_tiles.reshape(27, -1, 2, LANES),
        pick,
        preferred_element_type=jnp.float32,
    ).astype(jnp.bfloat16)
    mix_rows = gather(mix_part)

    wide_frames = with_columns(frames)
    wide_cot = with_columns(cotangent)
    long_frames = jnp.concatenate(
        (shift(wide_frames[-2:], PLANES, 1), wide_frames, shift(wide_frames[:1], PLANES, -1)),
        axis=0,
    )
    long_cot = jnp.concatenate((wide_cot, shift(wide_cot[:3], PLANES, -1)), axis=0)
    fields = jnp.stack((long_frames, cross(long_frames)))
    cots = jnp.stack((long_cot, cross(long_cot)))

    up_swapped = swap(up_rows)
    up_low = jnp.where(core == 0, up_rows, up_swapped)
    up_high = jnp.where(core == 0, up_swapped, up_rows)
    up_all = jnp.concatenate((up_low, up_high[:, 2 * up_half - up_count :]), axis=1)
    up_taps = up_all.reshape(planes_y, 3, 3, 3, in_channels // LANES, half // planes_y, LANES)
    up_forward = up_taps.transpose(1, 2, 3, 4, 6, 0, 5).reshape(3, 3, 3, in_channels, half)
    up_backward = up_taps.transpose(1, 2, 3, 0, 5, 4, 6).reshape(3, 3, 3, half, in_channels)

    even = convolve(fields, jnp.stack((up_forward[2], up_forward[0])))
    odd = convolve(fields[:, 1 : frame_count + 2], up_forward[1:2])
    odd = jnp.pad(odd, ((0, 0), (0, 1), (0, 0), (0, 0), (0, 0)))
    before = jnp.stack((even, odd), axis=2).reshape(2, -1, *even.shape[2:])[:, :-1]

    columns = lax.axis_size(COLS) * width
    firsts = jnp.stack((2 * xl + core, 2 * (1 - xl) + core)) * width - 1
    place = firsts[:, None] + jnp.arange(width + 2)
    inside = ((place >= 0) & (place < columns))[:, None, None, :, None]

    sigma = jax.nn.sigmoid(before)
    hidden = jnp.where(inside, before * sigma, 0.0)[:, :-1].astype(jnp.bfloat16)

    mix_swapped = swap(mix_rows)
    mix_low = jnp.where(core == 0, mix_rows, mix_swapped)
    mix_high = jnp.where(core == 0, mix_swapped, mix_rows)
    mix_all = jnp.stack((mix_low, mix_high), axis=2)
    mix_taps = mix_all.transpose(1, 0, 2, 3, 4).reshape(3, 3, 3, out_channels, half)

    decoded_parts = convolve(hidden, mix_taps.transpose(0, 1, 2, 4, 3))
    decoded_other = cross(decoded_parts[1].astype(jnp.bfloat16))

    hidden_grad = convolve(cots, mix_taps[::-1, ::-1, ::-1])
    late, sigma = before[:, 2:], sigma[:, 2:]
    slope = sigma * (1.0 + late * (1.0 - sigma))
    before_grad = jnp.where(inside, hidden_grad * slope, 0.0).astype(jnp.bfloat16)
    grad_parts = convolve(before_grad, up_backward[:, ::-1, ::-1], (2, 1, 1))
    grad_other = cross(grad_parts[1].astype(jnp.bfloat16))

    decoded = decoded_parts[0] + decoded_other.astype(jnp.float32)
    frames_grad = grad_parts[0] + grad_other.astype(jnp.float32)
    return decoded.astype(jnp.bfloat16), frames_grad.astype(jnp.bfloat16)


def solution(mesh):
    planes, columns = mesh.devices.shape
    shape = (4, 2, planes // 8, 2, columns // 2)
    fine = Mesh(mesh.devices.reshape(shape), (*PLANES, *COLS))
    placed = P(PLANES, None, COLS, None)
    weights = P(None, PLANES)
    return jax.shard_map(
        shards,
        mesh=fine,
        in_specs=(placed, weights, weights, placed),
        out_specs=(placed, placed),
        check_vma=False,
    )
```

time: 544 us -> 211 us (0.39)
  the two profiles are of different devices: /device:TPU:1 before, /device:TPU:30 now
where the time goes in v1:
time: 211 us; the launch traced here: 209 us
  starting transfers between devices  76.2 us (36%)
  waiting for transfers between devices  57.3 us (27%)
  local copies, waits for them, and re-layouts  52.3 us (25%)
  matrix products  13.4 us (6%)
  other arithmetic  8.52 us (4%)
    all_to_all x4, waiting for transfers between devices, spread(): lax.all_to_all(jnp.broadcast_to(array, (count, *array.shape)), axis, 0, 0...  43.1 us
    all_to_all x4, starting transfers between devices, spread(): lax.all_to_all(jnp.broadcast_to(array, (count, *array.shape)), axis, 0, 0...  30.4 us
    ppermute x7, starting transfers between devices, shift(): return lax.ppermute(array, axis, pairs)  23.2 us
    ppermute x5, starting transfers between devices, cross(): return lax.ppermute(array, ('xh', 'xl'), [(0, 3), (3, 0), (1, 2), (2, 1)])  18.8 us
    slice x7, local copies, waits for them, and re-layouts, shards(): even = convolve(fields, jnp.stack((up_forward[2], up_forward[0])))  15.3 us
    ppermute x5, waiting for transfers between devices, cross(): return lax.ppermute(array, ('xh', 'xl'), [(0, 3), (3, 0), (1, 2), (2, 1)])  14.3 us
    conv_general_dilated x5, matrix products, convolve(): lax.conv_general_dilated(field, kernel, strides, ((0, 0), (1, 1), (0, 0))...  13.2 us
    conv_general_dilated x15, local copies, waits for them, and re-layouts, convolve(): lax.conv_general_dilated(field, kernel, strides, ((0, 0), (1, 1), (0, 0))...  8.75 us
  transfers between devices with their start and end apart: 18, of which 7 were waited for; matrix products, arithmetic and copies ran while one was open for 16% of the time, Pallas kernels for 0%

profile of v1, /device:TPU:30, one launch (start us, length us, event | category | flops | bytes accessed | tf_op | source)
XLA Modules:
  0.0 209.2 jit_solution(2373786500259299082)
XLA Ops:
  1.4 2.4 %collective-permute-start.6 = (bf16[54,2,128]{2,0,1:T(8,128)(2,1)S(1)}, bf16[54,2,128]{2,0,1:T(8,128)(2,1)S(1)}, u32[]{:S(2)}, u32[]{:S(2)}) collective-permute-start(bf16[54,2,128]{2,0,1:T(8,128)(2,1)S(1)} %bitcast.155), channel_id=1, source_target_pairs={{0,66},{66,0},{2,64},{64,2},{1,67},{67,1},{3,65},{65,3},{4,70},{70... | collective-permute-start | bytes 82952 | tf_op jit(solution)/shard_map/ppermute | solution.py:18
  3.9 4.5 %collective-permute-done.6 = bf16[54,2,128]{2,0,1:T(8,128)(2,1)S(1)} collective-permute-done((bf16[54,2,128]{2,0,1:T(8,128)(2,1)S(1)}, bf16[54,2,128]{2,0,1:T(8,128)(2,1)S(1)}, u32[]{:S(2)}, u32[]{:S(2)}) %collective-permute-start.6) | collective-permute-done | bytes 27680 | tf_op jit(solution)/shard_map/ppermute | solution.py:18
  9.5 15.2 %all-to-all-start.2 = ((bf16[16,27,2,128]{3,2,1,0:T(2,128)(2,1)}), bf16[16,27,2,128]{3,2,1,0:T(2,128)(2,1)S(1)}, u32[]{:S(2)}, u32[]{:S(2)}) async-start(bf16[16,27,2,128]{3,2,1,0:T(2,128)(2,1)} %broadcast_in_dim.43), calls=%async_computation.2 | async-start | bytes 442368 | tf_op jit(solution)/shard_map/all_to_all | solution.py:27
  25.6 15.5 %all-to-all-done.2 = bf16[16,27,2,128]{3,2,1,0:T(2,128)(2,1)S(1)} async-done(((bf16[16,27,2,128]{3,2,1,0:T(2,128)(2,1)}), bf16[16,27,2,128]{3,2,1,0:T(2,128)(2,1)S(1)}, u32[]{:S(2)}, u32[]{:S(2)}) %all-to-all-start.2) | async-done | bytes 221216 | tf_op jit(solution)/shard_map/all_to_all | solution.py:27
  42.0 4.9 %all-to-all-start = ((bf16[16,41,2,128]{3,2,1,0:T(2,128)(2,1)}), bf16[16,41,2,128]{3,2,1,0:T(2,128)(2,1)S(1)}, u32[]{:S(2)}, u32[]{:S(2)}) async-start(bf16[16,41,2,128]{3,2,1,0:T(2,128)(2,1)} %broadcast_in_dim.40), calls=%async_computation | async-start | bytes 671744 | tf_op jit(solution)/shard_map/all_to_all | solution.py:27
  47.0 19.7 %all-to-all-done = bf16[16,41,2,128]{3,2,1,0:T(2,128)(2,1)S(1)} async-done(((bf16[16,41,2,128]{3,2,1,0:T(2,128)(2,1)}), bf16[16,41,2,128]{3,2,1,0:T(2,128)(2,1)S(1)}, u32[]{:S(2)}, u32[]{:S(2)}) %all-to-all-start) | async-done | bytes 335904 | tf_op jit(solution)/shard_map/all_to_all | solution.py:27
  66.7 1.0 broadcast_in_dim.44
  67.7 4.7 %all-to-all-start.3 = ((bf16[4,27,32,128]{3,2,1,0:T(8,128)(2,1)}), bf16[4,27,32,128]{3,2,1,0:T(8,128)(2,1)}, u32[]{:S(2)}, u32[]{:S(2)}) async-start(bf16[4,27,32,128]{3,2,1,0:T(8,128)(2,1)} %broadcast_in_dim.44), calls=%async_computation.3 | async-start | bytes 1769472 | tf_op jit(solution)/shard_map/all_to_all | solution.py:27
  72.6 7.9 %all-to-all-done.3 = bf16[4,27,32,128]{3,2,1,0:T(8,128)(2,1)} async-done(((bf16[4,27,32,128]{3,2,1,0:T(8,128)(2,1)}), bf16[4,27,32,128]{3,2,1,0:T(8,128)(2,1)}, u32[]{:S(2)}, u32[]{:S(2)}) %all-to-all-start.3) | async-done | bytes 884768 | tf_op jit(solution)/shard_map/all_to_all | solution.py:27
  80.6 1.3 broadcast_in_dim.41
  81.9 5.6 %all-to-all-start.1 = ((bf16[4,41,32,128]{3,2,1,0:T(8,128)(2,1)}), bf16[4,41,32,128]{3,2,1,0:T(8,128)(2,1)S(1)}, u32[]{:S(2)}, u32[]{:S(2)}) async-start(bf16[4,41,32,128]{3,2,1,0:T(8,128)(2,1)} %broadcast_in_dim.41), calls=%async_computation.1 | async-start | bytes 2686976 | tf_op jit(solution)/shard_map/all_to_all | solution.py:27
  87.5 1.9 collective-permute-start.1
  89.5 2.4 %collective-permute-start = (bf16[3,2,2,384]{3,2,1,0:T(2,128)(2,1)S(1)}, bf16[3,2,2,384]{3,2,1,0:T(2,128)(2,1)S(1)}, u32[]{:S(2)}, u32[]{:S(2)}) collective-permute-start(bf16[3,2,2,384]{3,2,1,0:T(2,128)(2,1)S(1)} %get-tuple-element.21), channel_id=1, source_target_pairs={{0,1},{1,2},{2,3},{4,5},{5,6},{6,7},{8,9},{9,10},{10,11},{12,13},{... | collective-permute-start | bytes 27656 | tf_op jit(solution)/shard_map/ppermute | solution.py:14
  91.9 3.2 %collective-permute-start.10 = (bf16[6,2,2,256]{3,2,1,0:T(2,128)(2,1)S(1)}, bf16[6,2,2,256]{3,2,1,0:T(2,128)(2,1)S(1)}, u32[]{:S(2)}, u32[]{:S(2)}) collective-permute-start(bf16[6,2,2,256]{3,2,1,0:T(2,128)(2,1)S(1)} %get-tuple-element.20), channel_id=1, source_target_pairs={{1,0},{2,1},{3,2},{5,4},{6,5},{7,6},{9,8},{10,9},{11,10},{13,12},{... | collective-permute-start | bytes 36872 | tf_op jit(solution)/shard_map/ppermute | solution.py:14
  95.1 1.9 collective-permute-start.9
  97.1 4.4 %collective-permute-start.3 = (bf16[1,2,28,384]{3,2,1,0:T(8,128)(2,1)S(1)}, bf16[1,2,28,384]{3,2,1,0:T(8,128)(2,1)S(1)}, u32[]{:S(2)}, u32[]{:S(2)}) collective-permute-start(bf16[1,2,28,384]{3,2,1,0:T(8,128)(2,1)S(1)} %pad_maximum_fusion.7), channel_id=1, source_target_pairs={{4,0},{8,4},{12,8},{16,12},{20,16},{24,20},{28,24},{32,28},{36,32}... | collective-permute-start | bytes 129032 | tf_op jit(solution)/shard_map/ppermute | solution.py:14
  101.6 1.9 collective-permute-start.2
  103.5 1.9 collective-permute-start.7
  105.5 7.5 %collective-permute-start.11 = (bf16[3,2,28,256]{3,2,1,0:T(8,128)(2,1)S(1)}, bf16[3,2,28,256]{3,2,1,0:T(8,128)(2,1)S(1)}, u32[]{:S(2)}, u32[]{:S(2)}) collective-permute-start(bf16[3,2,28,256]{3,2,1,0:T(8,128)(2,1)S(1)} %pad_maximum_fusion.5), channel_id=1, source_target_pairs={{4,0},{8,4},{12,8},{16,12},{20,16},{24,20},{28,24},{32,28},{36,32}... | collective-permute-start | bytes 258056 | tf_op jit(solution)/shard_map/ppermute | solution.py:14
  113.2 7.0 %collective-permute-start.4 = (bf16[6,2,28,384]{3,2,1,0:T(8,128)(2,1)S(1)}, bf16[6,2,28,384]{3,2,1,0:T(8,128)(2,1)S(1)}, u32[]{:S(2)}, u32[]{:S(2)}) collective-permute-start(bf16[6,2,28,384]{3,2,1,0:T(8,128)(2,1)S(1)} %pad_maximum_fusion.2), channel_id=1, source_target_pairs={{0,66},{66,0},{2,64},{64,2},{1,67},{67,1},{3,65},{65,3},{4,70},{70... | collective-permute-start | bytes 774152 | tf_op jit(solution)/shard_map/ppermute | solution.py:18
  121.1 2.1 collective-permute-start.12
  123.2 1.9 collective-permute-start.5
  126.0 1.6 collective-permute-done.4
  128.7 1.2 copy.106
  130.9 2.6 %collective-permute-done.12 = bf16[9,2,28,256]{3,2,1,0:T(8,128)(2,1)} collective-permute-done((bf16[9,2,28,256]{3,2,1,0:T(8,128)(2,1)}, bf16[9,2,28,256]{3,2,1,0:T(8,128)(2,1)}, u32[]{:S(2)}, u32[]{:S(2)}) %collective-permute-start.12) | collective-permute-done | bytes 258080 | tf_op jit(solution)/shard_map/ppermute | solution.py:18
  135.6 1.2 copy.128
  136.8 1.6 select_bitcast_fusion.1
  139.2 3.4 %convolution_select_fusion.2 = f32[7,2,16,4,128]{4,2,3,1,0:T(8,128)S(1)} fusion(bf16[3,3,3,256,128]{4,3,2,1,0:T(8,128)(2,1)S(1)} %bitcast.135, bf16[9,2,2,7,2,256]{5,3,2,4,1,0:T(8,128)(2,1)S(1)} %slice.122, bf16[9,2,2,8,4,256]{5,3,2,4,1,0:T(8,128)(2,1)S(1)} %copy.128, pred[16,4]{0,1:T(4,128)(4,1)S(1)} %copy-done.11), kind=kOutput, calls=%fused_computation.14 | convolution fusion | flops 1059733504 | bytes 3076160 | tf_op jit(solution)/shard_map/conv_general_dilated | solution.py:40
  144.1 1.4 fusion.64
  145.5 1.6 copy.114
  147.1 3.4 %slice.81 = bf16[1,3,3,384,128]{3,4,2,1,0:T(8,128)(2,1)} reshape(bf16[1,3,3,3,128,4,32]{4,3,6,5,2,1,0:T(4,128)(2,1)} %copy.114) | data formatting | bytes 1769472 | tf_op jit(solution)/shard_map/slice | solution.py:108
  150.5 2.5 %convolution_select_fusion.3 = f32[4,2,16,4,128]{4,2,3,1,0:T(8,128)S(1)} fusion(bf16[1,3,3,384,128]{3,4,2,1,0:T(8,128)(2,1)} %slice.81, bf16[6,2,2,7,2,384]{5,3,2,4,1,0:T(8,128)(2,1)} %slice.106, bf16[6,2,2,8,4,384]{5,3,2,4,1,0:T(8,128)(2,1)} %copy-done.4, pred[16,4]{0,1:T(4,128)(4,1)S(1)} %copy-done.11), kind=kOutput, calls=%fused_computation.16 | convolution fusion | flops 304709632 | bytes 1994816 | tf_op jit(solution)/shard_map/conv_general_dilated | solution.py:40
  153.8 1.6 copy.110
  155.4 2.6 %slice.79 = bf16[1,3,3,384,128]{3,4,2,1,0:T(8,128)(2,1)S(1)} reshape(bf16[1,3,3,3,128,4,32]{4,3,6,5,2,1,0:T(4,128)(2,1)} %copy.110) | data formatting | bytes 1769472 | tf_op jit(solution)/shard_map/slice | solution.py:107
  158.0 2.2 %copy.112 = bf16[1,3,3,384,128]{4,3,2,1,0:T(8,128)(2,1)} copy(bf16[1,3,3,384,128]{3,4,2,1,0:T(8,128)(2,1)S(1)} %slice.79) | data formatting | bytes 1769472 | tf_op jit(solution)/shard_map/slice | solution.py:107
  160.2 2.8 %copy.109 = bf16[1,3,3,3,128,4,32]{4,3,6,5,2,1,0:T(4,128)(2,1)} copy(bf16[1,3,3,3,128,4,32]{4,6,3,2,1,0,5:T(8,128)(2,1)} %get-tuple-element.10) | data formatting | bytes 1769472 | tf_op jit(solution)/shard_map/slice | solution.py:107
  163.0 2.6 %slice.77 = bf16[1,3,3,384,128]{3,4,2,1,0:T(8,128)(2,1)S(1)} reshape(bf16[1,3,3,3,128,4,32]{4,3,6,5,2,1,0:T(4,128)(2,1)} %copy.109) | data formatting | bytes 1769472 | tf_op jit(solution)/shard_map/slice | solution.py:107
  165.6 2.2 %copy.111 = bf16[1,3,3,384,128]{4,3,2,1,0:T(8,128)(2,1)} copy(bf16[1,3,3,384,128]{3,4,2,1,0:T(8,128)(2,1)S(1)} %slice.77) | data formatting | bytes 1769472 | tf_op jit(solution)/shard_map/slice | solution.py:107
  167.8 4.2 %fusion.6 = f32[5,2,16,4,128]{4,2,3,1,0:T(8,128)S(1)} fusion(bf16[1,3,3,384,128]{4,3,2,1,0:T(8,128)(2,1)} %copy.112, bf16[1,3,3,384,128]{4,3,2,1,0:T(8,128)(2,1)} %copy.111, bf16[6,2,2,7,2,384]{5,3,2,4,1,0:T(8,128)(2,1)} %slice.106, bf16[6,2,2,8,4,384]{5,3,2,4,1,0:T(8,128)(2,1)} %copy-done.4, pred[16,4]{0,1:T(4,128)(4,1)S(1)} %copy-done.11), kind=kOutput, calls=%fused_computation.15 | convolution fusion | flops 761249792 | bytes 2945088 | tf_op jit(solution)/shard_map/conv_general_dilated | solution.py:40
  174.9 1.6 fusion.68
  177.1 1.0 slice_bitcast_fusion
  178.9 5.1 %collective-permute-start.8 = (bf16[6,2,24,256]{3,1,2,0:T(2,128)(2,1)S(1)}, bf16[6,2,24,256]{3,1,2,0:T(2,128)(2,1)S(1)}, u32[]{:S(2)}, u32[]{:S(2)}) collective-permute-start(bf16[6,2,24,256]{3,1,2,0:T(2,128)(2,1)S(1)} %slice_bitcast_fusion.6), channel_id=1, source_target_pairs={{0,66},{66,0},{2,64},{64,2},{1,67},{67,1},{3,65},{65,3},{4,70},{70... | collective-permute-start | bytes 442376 | tf_op jit(solution)/shard_map/ppermute | solution.py:18
  184.0 4.5 %copy.133 = bf16[3,3,3,4,32,3,128]{6,5,4,3,2,1,0:T(4,128)(2,1)} copy(bf16[3,3,3,4,32,3,128]{6,4,5,2,1,0,3:T(8,128)(2,1)S(1)} %bitcast.134) | data formatting | bytes 5308416 | tf_op jit(solution)/shard_map/transpose | solution.py:105
  188.5 6.5 %reshape.129 = bf16[3,3,3,128,384]{4,3,2,1,0:T(8,128)(2,1)S(1)} reshape(bf16[3,3,3,4,32,3,128]{6,5,4,3,2,1,0:T(4,128)(2,1)} %copy.133) | data formatting | bytes 5308416 | tf_op jit(solution)/shard_map/reshape | solution.py:105
  195.0 1.6 fusion.39
  197.1 1.5 fusion.69
  199.7 2.2 %collective-permute-start.13 = (bf16[3,2,24,384]{3,1,2,0:T(2,128)(2,1)S(1)}, bf16[3,2,24,384]{3,1,2,0:T(2,128)(2,1)S(1)}, u32[]{:S(2)}, u32[]{:S(2)}) collective-permute-start(bf16[3,2,24,384]{3,1,2,0:T(2,128)(2,1)S(1)} %slice_bitcast_fusion.7), channel_id=1, source_target_pairs={{0,66},{66,0},{2,64},{64,2},{1,67},{67,1},{3,65},{65,3},{4,70},{70... | collective-permute-start | bytes 331784 | tf_op jit(solution)/shard_map/ppermute | solution.py:18
  202.1 5.5 %collective-permute-done.13 = bf16[3,2,24,384]{3,1,2,0:T(2,128)(2,1)S(1)} collective-permute-done((bf16[3,2,24,384]{3,1,2,0:T(2,128)(2,1)S(1)}, bf16[3,2,24,384]{3,1,2,0:T(2,128)(2,1)S(1)}, u32[]{:S(2)}, u32[]{:S(2)}) %collective-permute-start.13) | collective-permute-done | bytes 110624 | tf_op jit(solution)/shard_map/ppermute | solution.py:18
  (105 shorter events, 20.8 us)
Async XLA Ops:
  1.4 7.0 %collective-permute-start.6 = (bf16[54,2,128]{2,0,1:T(8,128)(2,1)S(1)}, bf16[54,2,128]{2,0,1:T(8,128)(2,1)S(1)}, u32[]{:S(2)}, u32[]{:S(2)}) collective-permute-start(bf16[54,2,128]{2,0,1:T(8,128)(2,1)S(1)} %bitcast.155), channel_id=1, source_target_pairs={{0,66},{66,0},{2,64},{64,2},{1,67},{67,1},{3,65},{65,3},{4,70},{70... | collective-permute-start | bytes 82952 | tf_op jit(solution)/shard_map/ppermute | solution.py:18
  9.5 31.6 %all-to-all-start.2 = ((bf16[16,27,2,128]{3,2,1,0:T(2,128)(2,1)}), bf16[16,27,2,128]{3,2,1,0:T(2,128)(2,1)S(1)}, u32[]{:S(2)}, u32[]{:S(2)}) async-start(bf16[16,27,2,128]{3,2,1,0:T(2,128)(2,1)} %broadcast_in_dim.43), calls=%async_computation.2 | async-start | bytes 442368 | tf_op jit(solution)/shard_map/all_to_all | solution.py:27
  42.0 24.7 %all-to-all-start = ((bf16[16,41,2,128]{3,2,1,0:T(2,128)(2,1)}), bf16[16,41,2,128]{3,2,1,0:T(2,128)(2,1)S(1)}, u32[]{:S(2)}, u32[]{:S(2)}) async-start(bf16[16,41,2,128]{3,2,1,0:T(2,128)(2,1)} %broadcast_in_dim.40), calls=%async_computation | async-start | bytes 671744 | tf_op jit(solution)/shard_map/all_to_all | solution.py:27
  67.7 12.8 %all-to-all-start.3 = ((bf16[4,27,32,128]{3,2,1,0:T(8,128)(2,1)}), bf16[4,27,32,128]{3,2,1,0:T(8,128)(2,1)}, u32[]{:S(2)}, u32[]{:S(2)}) async-start(bf16[4,27,32,128]{3,2,1,0:T(8,128)(2,1)} %broadcast_in_dim.44), calls=%async_computation.3 | async-start | bytes 1769472 | tf_op jit(solution)/shard_map/all_to_all | solution.py:27
  80.6 6.9 %copy-start.3 = (bf16[3,2,24,384]{3,2,1,0:T(8,128)(2,1)S(1)}, bf16[3,2,24,384]{3,2,1,0:T(8,128)(2,1)}, u32[]{:S(2)}) copy-start(bf16[3,2,24,384]{3,2,1,0:T(8,128)(2,1)} %param.4) | copy-start | bytes 331780
  81.9 10.0 %copy-start.8 = (bf16[6,2,24,256]{3,2,1,0:T(8,128)(2,1)S(1)}, bf16[6,2,24,256]{3,2,1,0:T(8,128)(2,1)}, u32[]{:S(2)}) copy-start(bf16[6,2,24,256]{3,2,1,0:T(8,128)(2,1)} %param.7) | copy-start | bytes 442372
  81.9 41.4 %all-to-all-start.1 = ((bf16[4,41,32,128]{3,2,1,0:T(8,128)(2,1)}), bf16[4,41,32,128]{3,2,1,0:T(8,128)(2,1)S(1)}, u32[]{:S(2)}, u32[]{:S(2)}) async-start(bf16[4,41,32,128]{3,2,1,0:T(8,128)(2,1)} %broadcast_in_dim.41), calls=%async_computation.1 | async-start | bytes 2686976 | tf_op jit(solution)/shard_map/all_to_all | solution.py:27
  87.5 9.6 %collective-permute-start.1 = (bf16[3,2,2,384]{3,2,1,0:T(2,128)(2,1)S(1)}, bf16[3,2,2,384]{3,2,1,0:T(2,128)(2,1)S(1)}, u32[]{:S(2)}, u32[]{:S(2)}) collective-permute-start(bf16[3,2,2,384]{3,2,1,0:T(2,128)(2,1)S(1)} %get-tuple-element.22), channel_id=1, source_target_pairs={{1,0},{2,1},{3,2},{5,4},{6,5},{7,6},{9,8},{10,9},{11,10},{13,12},{... | collective-permute-start | bytes 27656 | tf_op jit(solution)/shard_map/ppermute | solution.py:14
  89.5 7.6 %collective-permute-start = (bf16[3,2,2,384]{3,2,1,0:T(2,128)(2,1)S(1)}, bf16[3,2,2,384]{3,2,1,0:T(2,128)(2,1)S(1)}, u32[]{:S(2)}, u32[]{:S(2)}) collective-permute-start(bf16[3,2,2,384]{3,2,1,0:T(2,128)(2,1)S(1)} %get-tuple-element.21), channel_id=1, source_target_pairs={{0,1},{1,2},{2,3},{4,5},{5,6},{6,7},{8,9},{9,10},{10,11},{12,13},{... | collective-permute-start | bytes 27656 | tf_op jit(solution)/shard_map/ppermute | solution.py:14
  91.9 13.5 %collective-permute-start.10 = (bf16[6,2,2,256]{3,2,1,0:T(2,128)(2,1)S(1)}, bf16[6,2,2,256]{3,2,1,0:T(2,128)(2,1)S(1)}, u32[]{:S(2)}, u32[]{:S(2)}) collective-permute-start(bf16[6,2,2,256]{3,2,1,0:T(2,128)(2,1)S(1)} %get-tuple-element.20), channel_id=1, source_target_pairs={{1,0},{2,1},{3,2},{5,4},{6,5},{7,6},{9,8},{10,9},{11,10},{13,12},{... | collective-permute-start | bytes 36872 | tf_op jit(solution)/shard_map/ppermute | solution.py:14
  95.1 10.4 %collective-permute-start.9 = (bf16[6,2,2,256]{3,2,1,0:T(2,128)(2,1)S(1)}, bf16[6,2,2,256]{3,2,1,0:T(2,128)(2,1)S(1)}, u32[]{:S(2)}, u32[]{:S(2)}) collective-permute-start(bf16[6,2,2,256]{3,2,1,0:T(2,128)(2,1)S(1)} %get-tuple-element.19), channel_id=1, source_target_pairs={{0,1},{1,2},{2,3},{4,5},{5,6},{6,7},{8,9},{9,10},{10,11},{12,13},{... | collective-permute-start | bytes 36872 | tf_op jit(solution)/shard_map/ppermute | solution.py:14
  97.1 16.0 %copy-start.10 = (bf16[3,2,2,384]{3,2,1,0:T(2,128)(2,1)}, bf16[3,2,2,384]{3,2,1,0:T(2,128)(2,1)S(1)}, u32[]{:S(2)}) copy-start(bf16[3,2,2,384]{3,2,1,0:T(2,128)(2,1)S(1)} %collective-permute-done) | copy-start | bytes 27652
  97.1 15.9 %collective-permute-start.3 = (bf16[1,2,28,384]{3,2,1,0:T(8,128)(2,1)S(1)}, bf16[1,2,28,384]{3,2,1,0:T(8,128)(2,1)S(1)}, u32[]{:S(2)}, u32[]{:S(2)}) collective-permute-start(bf16[1,2,28,384]{3,2,1,0:T(8,128)(2,1)S(1)} %pad_maximum_fusion.7), channel_id=1, source_target_pairs={{4,0},{8,4},{12,8},{16,12},{20,16},{24,20},{28,24},{32,28},{36,32}... | collective-permute-start | bytes 129032 | tf_op jit(solution)/shard_map/ppermute | solution.py:14
  101.6 11.5 %collective-permute-start.2 = (bf16[2,2,28,384]{3,2,1,0:T(8,128)(2,1)S(1)}, bf16[2,2,28,384]{3,2,1,0:T(8,128)(2,1)S(1)}, u32[]{:S(2)}, u32[]{:S(2)}) collective-permute-start(bf16[2,2,28,384]{3,2,1,0:T(8,128)(2,1)S(1)} %slice.105), channel_id=1, source_target_pairs={{0,4},{4,8},{8,12},{12,16},{16,20},{20,24},{24,28},{28,32},{32,36}... | collective-permute-start | bytes 258056 | tf_op jit(solution)/shard_map/ppermute | solution.py:14
  103.5 33.3 %collective-permute-start.7 = (bf16[4,27,32,128]{3,2,1,0:T(8,128)(2,1)}, bf16[4,27,32,128]{3,2,1,0:T(8,128)(2,1)}, u32[]{:S(2)}, u32[]{:S(2)}) collective-permute-start(bf16[4,27,32,128]{3,2,1,0:T(8,128)(2,1)} %all-to-all-done.3), channel_id=1, source_target_pairs={{0,1},{1,0},{2,3},{3,2},{4,5},{5,4},{6,7},{7,6},{8,9},{9,8},{10,11... | collective-permute-start | bytes 2654216 | tf_op jit(solution)/shard_map/ppermute | solution.py:22
  105.5 14.7 %collective-permute-start.11 = (bf16[3,2,28,256]{3,2,1,0:T(8,128)(2,1)S(1)}, bf16[3,2,28,256]{3,2,1,0:T(8,128)(2,1)S(1)}, u32[]{:S(2)}, u32[]{:S(2)}) collective-permute-start(bf16[3,2,28,256]{3,2,1,0:T(8,128)(2,1)S(1)} %pad_maximum_fusion.5), channel_id=1, source_target_pairs={{4,0},{8,4},{12,8},{16,12},{20,16},{24,20},{28,24},{32,28},{36,32}... | collective-permute-start | bytes 258056 | tf_op jit(solution)/shard_map/ppermute | solution.py:14
  113.2 14.4 %collective-permute-start.4 = (bf16[6,2,28,384]{3,2,1,0:T(8,128)(2,1)S(1)}, bf16[6,2,28,384]{3,2,1,0:T(8,128)(2,1)S(1)}, u32[]{:S(2)}, u32[]{:S(2)}) collective-permute-start(bf16[6,2,28,384]{3,2,1,0:T(8,128)(2,1)S(1)} %pad_maximum_fusion.2), channel_id=1, source_target_pairs={{0,66},{66,0},{2,64},{64,2},{1,67},{67,1},{3,65},{65,3},{4,70},{70... | collective-permute-start | bytes 774152 | tf_op jit(solution)/shard_map/ppermute | solution.py:18
  121.1 12.4 %collective-permute-start.12 = (bf16[9,2,28,256]{3,2,1,0:T(8,128)(2,1)}, bf16[9,2,28,256]{3,2,1,0:T(8,128)(2,1)}, u32[]{:S(2)}, u32[]{:S(2)}) collective-permute-start(bf16[9,2,28,256]{3,2,1,0:T(8,128)(2,1)} %get-tuple-element.18), channel_id=1, source_target_pairs={{0,66},{66,0},{2,64},{64,2},{1,67},{67,1},{3,65},{65,3},{4,70},{70... | collective-permute-start | bytes 774152 | tf_op jit(solution)/shard_map/ppermute | solution.py:18
  123.2 20.3 %collective-permute-start.5 = (bf16[4,41,32,128]{3,2,1,0:T(8,128)(2,1)S(1)}, bf16[4,41,32,128]{3,2,1,0:T(8,128)(2,1)S(1)}, u32[]{:S(2)}, u32[]{:S(2)}) collective-permute-start(bf16[4,41,32,128]{3,2,1,0:T(8,128)(2,1)S(1)} %all-to-all-done.1), channel_id=1, source_target_pairs={{0,1},{1,0},{2,3},{3,2},{4,5},{5,4},{6,7},{7,6},{8,9},{9,8},{10,11... | collective-permute-start | bytes 4030472 | tf_op jit(solution)/shard_map/ppermute | solution.py:22
  128.7 4.8 %copy-start.6 = (bf16[1,9,2,28,256]{4,3,2,1,0:T(8,128)(2,1)S(1)}, bf16[1,9,2,28,256]{4,3,2,1,0:T(8,128)(2,1)}, u32[]{:S(2)}) copy-start(bf16[1,9,2,28,256]{4,3,2,1,0:T(8,128)(2,1)} %get-tuple-element.17) | copy-start | bytes 774148
  130.0 3.6 %copy-start.4 = (bf16[6,2,2,8,4,384]{5,3,2,4,1,0:T(8,128)(2,1)}, bf16[6,2,2,8,4,384]{5,3,2,4,1,0:T(8,128)(2,1)S(1)}, u32[]{:S(2)}) copy-start(bf16[6,2,2,8,4,384]{5,3,2,4,1,0:T(8,128)(2,1)S(1)} %copy.106) | copy-start | bytes 1769476
  138.6 0.7 copy-start.11
  139.1 3.5 %copy-start = (bf16[27,4,2,32,128]{4,3,2,1,0:T(8,128)(2,1)}, bf16[27,4,2,32,128]{4,3,2,1,0:T(8,128)(2,1)S(1)}, u32[]{:S(2)}) copy-start(bf16[27,4,2,32,128]{4,3,2,1,0:T(8,128)(2,1)S(1)} %copy.123) | copy-start | bytes 5308420
  167.8 4.3 %copy-start.7 = (f32[4,2,16,4,128]{4,3,2,1,0:T(4,128)S(1)}, f32[4,2,16,4,128]{4,3,2,1,0:T(4,128)}, u32[]{:S(2)}) copy-start(f32[4,2,16,4,128]{4,3,2,1,0:T(4,128)} %copy.143) | copy-start | bytes 786436
  173.2 0.8 copy-start.2
  173.2 1.7 copy-start.1
  173.3 1.6 copy-start.9
  178.9 29.4 %collective-permute-start.8 = (bf16[6,2,24,256]{3,1,2,0:T(2,128)(2,1)S(1)}, bf16[6,2,24,256]{3,1,2,0:T(2,128)(2,1)S(1)}, u32[]{:S(2)}, u32[]{:S(2)}) collective-permute-start(bf16[6,2,24,256]{3,1,2,0:T(2,128)(2,1)S(1)} %slice_bitcast_fusion.6), channel_id=1, source_target_pairs={{0,66},{66,0},{2,64},{64,2},{1,67},{67,1},{3,65},{65,3},{4,70},{70... | collective-permute-start | bytes 442376 | tf_op jit(solution)/shard_map/ppermute | solution.py:18
  198.7 9.7 %copy-start.5 = (f32[2,6,2,24,256]{4,2,3,0,1:T(2,128)S(1)}, f32[2,6,2,24,256]{4,2,3,0,1:T(2,128)}, u32[]{:S(2)}) copy-start(f32[2,6,2,24,256]{4,2,3,0,1:T(2,128)} %slice_bitcast_fusion) | copy-start | bytes 1769476
  199.7 7.9 %collective-permute-start.13 = (bf16[3,2,24,384]{3,1,2,0:T(2,128)(2,1)S(1)}, bf16[3,2,24,384]{3,1,2,0:T(2,128)(2,1)S(1)}, u32[]{:S(2)}, u32[]{:S(2)}) collective-permute-start(bf16[3,2,24,384]{3,1,2,0:T(2,128)(2,1)S(1)} %slice_bitcast_fusion.7), channel_id=1, source_target_pairs={{0,66},{66,0},{2,64},{64,2},{1,67},{67,1},{3,65},{65,3},{4,70},{70... | collective-permute-start | bytes 331784 | tf_op jit(solution)/shard_map/ppermute | solution.py:18
